TPU v7x, 512 devices: a whole 4x8x8 slice. The times are simulated.
512 devices in a mesh: row: 16 (over y, core), col: 32 (over z, x).
Axes of the slice: x: 4, y: 8, z: 8, core: 2. Of those that a mesh axis runs over, the one named last changes fastest.
Arguments:
- a_vals: bfloat16 [2, 32, 64, 5, 128, 128], P(None, 'row', 'col'), may hold values from -0.5 to 0.5
- a_off: int32 [2, 32, 64, 5], P(None, 'row', 'col'), may hold values from 0 to 8, as said below
- a_count: int32 [2, 32, 64], P(None, 'row', 'col'), may hold values from 1 to 5
- p_vals: bfloat16 [32, 64, 4, 128, 128], P('row', 'col'), may hold values from -1.1953125 to 1.1953125
Outputs:
- coarse: bfloat16 [2, 16, 32, 25, 128, 128], P(None, 'row', 'col')
Inputs may be any that keep to these rules, and one draw needn't show every extreme that they name: Each row of a_off lists 5 different stencil positions of 0 to 8.
All inputs are finite; a program needn't handle non-finite values.
Results may differ from a plain program's by a relative error of at most 0.0049.
Values may be sent and summed in bfloat16 or wider, within the bound.
A program may use at most 64 MiB of HBM per device.

v0:
```python
import jax
import jax.numpy as jnp
from jax import lax
from jax.sharding import PartitionSpec as P


def padded(block, sides, width):
    for axis, dim in sides:
        count = lax.axis_size(axis)
        forward = [(i, i + 1) for i in range(count - 1)]
        forward.append((count - 1, 0))
        backward = [(target, source) for source, target in forward]
        low = lax.ppermute(
            lax.slice_in_dim(block, block.shape[dim] - width, None, axis=dim), axis, forward
        )
        high = lax.ppermute(lax.slice_in_dim(block, 0, width, axis=dim), axis, backward)
        block = jnp.concatenate([low, block, high], axis=dim)
    return block


def corner_of(lag):
    return 1 if lag in (-1, 2) else 0


def shift_groups():
    lags = [(lag_x, lag_y) for lag_x in range(-1, 3) for lag_y in range(-1, 3)]
    result = []
    for place_x in range(3):
        for place_y in range(3):
            members = [
                (lag_x, lag_y, 2 * corner_of(lag_x) + corner_of(lag_y))
                for lag_x, lag_y in lags
                if lag_x // 2 + 1 == place_x and lag_y // 2 + 1 == place_y
            ]
            result = result + [((place_x, place_y), members)]
    return result


def band_index(near, anchor, corner):
    return (
        jnp.floor_divide(near, 2)
        + corner * (2 * jnp.remainder(near, 2) - 1)
        - jnp.floor_divide(anchor, 2)
        + 1
    )


def products_of_rows(blocks, slot_offsets, p_window, margin):
    rows_x, rows_y = (blocks.shape[0], blocks.shape[1])
    window_y = p_window.shape[1]
    p_flat = p_window.reshape((p_window.shape[0] * window_y,) + p_window.shape[2:])
    anchor_x = jnp.arange(rows_x, dtype=jnp.int32)[:, None, None]
    anchor_y = jnp.arange(rows_y, dtype=jnp.int32)[None, :, None]
    near_x = anchor_x + slot_offsets // 3 - 1
    near_y = anchor_y + slot_offsets % 3 - 1
    position = (near_x + margin) * window_y + (near_y + margin)
    picked = p_flat[position]
    quadrants = jnp.arange(4, dtype=jnp.int32)
    band = band_index(near_x[..., None], anchor_x[..., None], quadrants // 2) * 3 + band_index(
        near_y[..., None], anchor_y[..., None], quadrants % 2
    )
    onehot = (band[..., None] == jnp.arange(9, dtype=jnp.int32)).astype(jnp.bfloat16)
    selected = jnp.einsum(
        "xykqj,xykqbc->xykjbc", onehot, picked, preferred_element_type=jnp.bfloat16
    )
    summed = jnp.einsum("xykab,xykjbc->xyjac", blocks, selected, preferred_element_type=jnp.float32)
    return summed.astype(jnp.bfloat16)


def assemble(w_window, p_window, w_margin, p_margin):
    operators = w_window.shape[0]
    block = p_window.shape[-1]
    total = jnp.zeros((operators, 5, 5, block, block), jnp.float32)
    for place, members in shift_groups():
        p_rows = jnp.stack(
            [
                p_window[lag_x + p_margin, lag_y + p_margin, quadrant]
                for lag_x, lag_y, quadrant in members
            ]
        )
        w_rows = jnp.stack(
            [w_window[:, lag_x + w_margin, lag_y + w_margin] for lag_x, lag_y, quadrant in members],
            axis=1,
        )
        partial_terms = jnp.einsum(
            "uab,sujac->sjbc", p_rows, w_rows, preferred_element_type=jnp.float32
        )
        partial_terms = partial_terms.reshape((operators, 3, 3, block, block))
        total = total.at[:, place[0] : place[0] + 3, place[1] : place[1] + 3].add(partial_terms)
    return total.reshape((operators, 25, block, block)).astype(jnp.bfloat16)[:, None, None]


def per_device(a_vals, a_off, a_count, p_vals):
    slot_total = a_vals.shape[3]
    operators = a_vals.shape[0]
    alive = (jnp.arange(slot_total, dtype=jnp.int32) < a_count[..., None]).astype(jnp.bfloat16)
    a_live = a_vals * alive[..., None, None]
    p_window = padded(p_vals, (("row", 0), ("col", 1)), 1)
    w_own = jnp.stack(
        [
            products_of_rows(a_live[operator], a_off[operator], p_window, 1)
            for operator in range(operators)
        ]
    )
    w_window = padded(w_own, (("row", 1), ("col", 2)), 1)
    return assemble(w_window, p_window, 1, 1)


def solution(mesh):
    placed = (
        P(None, "row", "col", None, None, None),
        P(None, "row", "col", None),
        P(None, "row", "col"),
        P("row", "col", None, None, None),
    )
    return jax.shard_map(
        per_device,
        mesh=mesh,
        in_specs=placed,
        out_specs=P(None, "row", "col", None, None, None),
        check_vma=False,
    )
```

profile of v0, /device:TPU:25, one launch (start us, length us, event | category | flops | bytes accessed | tf_op | source)
XLA Modules:
  0.0 155.6 jit_solution(3545787794502407112)
XLA Ops:
  0.0 1.1 fusion.107
  1.1 3.1 %collective-permute-start = (bf16[1,2,4,128,128]{4,3,2,1,0:T(8,128)(2,1)S(1)}, bf16[1,2,4,128,128]{4,3,2,1,0:T(8,128)(2,1)S(1)}, u32[]{:S(2)}, u32[]{:S(2)}) collective-permute-start(bf16[1,2,4,128,128]{4,3,2,1,0:T(8,128)(2,1)S(1)} %get-tuple-element.148), channel_id=1, source_target_pairs={{0,32},{32,64},{64,96},{96,128},{128,160},{160,192},{192,224},{224... | collective-permute-start | bytes 786440 | tf_op jit(solution)/shard_map/ppermute | solution.py:13
  6.6 0.9 collective-permute-done
  7.5 1.2 constant_dynamic-update-slice_fusion.1
  8.7 2.4 %collective-permute-done.1 = bf16[1,2,4,128,128]{4,3,2,1,0:T(8,128)(2,1)S(1)} collective-permute-done((bf16[1,2,4,128,128]{4,3,2,1,0:T(8,128)(2,1)S(1)}, bf16[1,2,4,128,128]{4,3,2,1,0:T(8,128)(2,1)S(1)}, u32[]{:S(2)}, u32[]{:S(2)}) %collective-permute-start.1) | collective-permute-done | bytes 262176 | tf_op jit(solution)/shard_map/ppermute | solution.py:16
  11.3 12.9 %collective-permute-start.3 = (bf16[4,1,4,128,128]{4,3,2,1,0:T(8,128)(2,1)S(1)}, bf16[4,1,4,128,128]{4,3,2,1,0:T(8,128)(2,1)S(1)}, u32[]{:S(2)}, u32[]{:S(2)}) collective-permute-start(bf16[4,1,4,128,128]{4,3,2,1,0:T(8,128)(2,1)S(1)} %get-tuple-element.138), channel_id=1, source_target_pairs={{1,0},{2,1},{3,2},{4,3},{5,4},{6,5},{7,6},{8,7},{9,8},{10,9},{11,1... | collective-permute-start | bytes 1572872 | tf_op jit(solution)/shard_map/ppermute | solution.py:16
  24.2 1.9 %collective-permute-start.2 = (bf16[4,1,4,128,128]{4,3,2,1,0:T(8,128)(2,1)S(1)}, bf16[4,1,4,128,128]{4,3,2,1,0:T(8,128)(2,1)S(1)}, u32[]{:S(2)}, u32[]{:S(2)}) collective-permute-start(bf16[4,1,4,128,128]{4,3,2,1,0:T(8,128)(2,1)S(1)} %get-tuple-element.137), channel_id=1, source_target_pairs={{0,1},{1,2},{2,3},{3,4},{4,5},{5,6},{6,7},{7,8},{8,9},{9,10},{10,1... | collective-permute-start | bytes 1572872 | tf_op jit(solution)/shard_map/ppermute | solution.py:13
  26.4 7.6 %collective-permute-done.3 = bf16[4,1,4,128,128]{4,3,2,1,0:T(8,128)(2,1)S(1)} collective-permute-done((bf16[4,1,4,128,128]{4,3,2,1,0:T(8,128)(2,1)S(1)}, bf16[4,1,4,128,128]{4,3,2,1,0:T(8,128)(2,1)S(1)}, u32[]{:S(2)}, u32[]{:S(2)}) %collective-permute-start.3) | collective-permute-done | bytes 524320 | tf_op jit(solution)/shard_map/ppermute | solution.py:16
  34.0 7.4 %collective-permute-done.2 = bf16[4,1,4,128,128]{4,3,2,1,0:T(8,128)(2,1)S(1)} collective-permute-done((bf16[4,1,4,128,128]{4,3,2,1,0:T(8,128)(2,1)S(1)}, bf16[4,1,4,128,128]{4,3,2,1,0:T(8,128)(2,1)S(1)}, u32[]{:S(2)}, u32[]{:S(2)}) %collective-permute-start.2) | collective-permute-done | bytes 524320 | tf_op jit(solution)/shard_map/ppermute | solution.py:13
  42.2 2.5 %gather_fusion = bf16[20,4,128,128]{3,2,1,0:T(8,128)(2,1)} fusion(bf16[16,4,128,128]{3,2,1,0:T(8,128)(2,1)S(1)} %bitcast.302, s32[1024]{0:T(1024)S(1)} %get-tuple-element.174), kind=kCustom, calls=%fused_computation | custom fusion | bytes 5242960 | tf_op jit(solution)/shard_map/gather | solution.py:57
  44.8 2.6 %gather_fusion.1 = bf16[20,4,128,128]{3,2,1,0:T(8,128)(2,1)} fusion(bf16[16,4,128,128]{3,2,1,0:T(8,128)(2,1)S(1)} %bitcast.303, s32[1024]{0:T(1024)S(1)} %get-tuple-element.173), kind=kCustom, calls=%fused_computation.1 | custom fusion | bytes 5242960 | tf_op jit(solution)/shard_map/gather | solution.py:57
  47.3 6.3 %fusion.6 = bf16[2,2,5,9,128,128]{5,3,4,2,1,0:T(8,128)(2,1)S(1)} fusion(bf16[2,2,5,4,128,128]{5,4,3,2,1,0:T(8,128)(2,1)} %bitcast.305, s32[2,2,5,4]{3,2,1,0:T(8,128)S(1)} %get-tuple-element.162), kind=kOutput, calls=%fused_computation.19 | convolution fusion | flops 23593680 | bytes 8520000 | tf_op jit(solution)/shard_map/xykqj,xykqbc->xykjbc/dot_general | solution.py:63
  53.6 2.3 %fusion.14 = bf16[1,2,2,9,128,128]{4,5,3,2,1,0:T(8,128)(2,1)S(1)} fusion(bf16[2,2,5,9,128,128]{5,3,4,2,1,0:T(8,128)(2,1)S(1)} %fusion.6, bf16[2,2,2,5,128,128]{5,4,3,2,1,0:T(8,128)(2,1)S(1)} %broadcast_multiply_fusion), kind=kOutput, calls=%fused_computation.28 | convolution fusion | flops 755564544 | bytes 12320768 | tf_op jit(solution)/shard_map/xykab,xykjbc->xyjac/dot_general | solution.py:66
  56.0 5.2 %fusion.4 = bf16[2,2,5,9,128,128]{5,3,4,2,1,0:T(8,128)(2,1)S(1)} fusion(bf16[2,2,5,4,128,128]{5,4,3,2,1,0:T(8,128)(2,1)S(1)} %bitcast.304, s32[2,2,5,4]{3,2,1,0:T(8,128)S(1)} %get-tuple-element.161), kind=kOutput, calls=%fused_computation.17 | convolution fusion | flops 23593680 | bytes 8520000 | tf_op jit(solution)/shard_map/xykqj,xykqbc->xykjbc/dot_general | solution.py:63
  61.2 2.3 %fusion.17 = bf16[1,2,2,9,128,128]{4,5,3,2,1,0:T(8,128)(2,1)S(1)} fusion(bf16[2,2,5,9,128,128]{5,3,4,2,1,0:T(8,128)(2,1)S(1)} %fusion.4, bf16[2,2,2,5,128,128]{5,4,3,2,1,0:T(8,128)(2,1)S(1)} %broadcast_multiply_fusion), kind=kOutput, calls=%fused_computation.29 | convolution fusion | flops 755564544 | bytes 12320768 | tf_op jit(solution)/shard_map/xykab,xykjbc->xyjac/dot_general | solution.py:66
  63.8 2.9 %collective-permute-start.4 = (bf16[2,1,2,9,128,128]{4,5,3,2,1,0:T(8,128)(2,1)S(1)}, bf16[2,1,2,9,128,128]{4,5,3,2,1,0:T(8,128)(2,1)S(1)}, u32[]{:S(2)}, u32[]{:S(2)}) collective-permute-start(bf16[2,1,2,9,128,128]{4,5,3,2,1,0:T(8,128)(2,1)S(1)} %get-tuple-element.131), channel_id=1, source_target_pairs={{0,32},{32,64},{64,96},{96,128},{128,160},{160,192},{192,224},{224... | collective-permute-start | bytes 3538952 | tf_op jit(solution)/shard_map/ppermute | solution.py:13
  68.7 11.9 %collective-permute-done.5 = bf16[2,1,2,9,128,128]{4,5,3,2,1,0:T(8,128)(2,1)S(1)} collective-permute-done((bf16[2,1,2,9,128,128]{4,5,3,2,1,0:T(8,128)(2,1)S(1)}, bf16[2,1,2,9,128,128]{4,5,3,2,1,0:T(8,128)(2,1)S(1)}, u32[]{:S(2)}, u32[]{:S(2)}) %collective-permute-start.5) | collective-permute-done | bytes 1179680 | tf_op jit(solution)/shard_map/ppermute | solution.py:16
  81.2 1.8 %fusion.105 = (bf16[2,4,1,9,128,128]{4,5,3,2,1,0:T(8,128)(2,1)S(1)}, bf16[2,4,1,9,128,128]{4,5,3,2,1,0:T(8,128)(2,1)S(1)}) fusion(bf16[2,4,2,9,128,128]{4,5,3,2,1,0:T(8,128)(2,1)S(1)} %pad_maximum_fusion), kind=kLoop, calls=%fused_computation.222 | loop fusion | bytes 9437184 | tf_op jit(solution)/shard_map/slice | solution.py:16
  83.0 1.9 %collective-permute-start.6 = (bf16[2,4,1,9,128,128]{4,5,3,2,1,0:T(8,128)(2,1)S(1)}, bf16[2,4,1,9,128,128]{4,5,3,2,1,0:T(8,128)(2,1)S(1)}, u32[]{:S(2)}, u32[]{:S(2)}) collective-permute-start(bf16[2,4,1,9,128,128]{4,5,3,2,1,0:T(8,128)(2,1)S(1)} %get-tuple-element.122), channel_id=1, source_target_pairs={{0,1},{1,2},{2,3},{3,4},{4,5},{5,6},{6,7},{7,8},{8,9},{9,10},{10,1... | collective-permute-start | bytes 7077896 | tf_op jit(solution)/shard_map/ppermute | solution.py:13
  85.0 0.8 slice_bitcast_fusion.39
  85.8 6.9 %collective-permute-start.7 = (bf16[2,4,1,9,128,128]{4,5,3,2,1,0:T(8,128)(2,1)S(1)}, bf16[2,4,1,9,128,128]{4,5,3,2,1,0:T(8,128)(2,1)S(1)}, u32[]{:S(2)}, u32[]{:S(2)}) collective-permute-start(bf16[2,4,1,9,128,128]{4,5,3,2,1,0:T(8,128)(2,1)S(1)} %get-tuple-element.121), channel_id=1, source_target_pairs={{1,0},{2,1},{3,2},{4,3},{5,4},{6,5},{7,6},{8,7},{9,8},{10,9},{11,1... | collective-permute-start | bytes 7077896 | tf_op jit(solution)/shard_map/ppermute | solution.py:16
  92.7 0.8 slice_bitcast_fusion.33
  95.3 0.8 slice_bitcast_fusion.29
  98.2 41.5 %collective-permute-done.6 = bf16[2,4,1,9,128,128]{4,5,3,2,1,0:T(8,128)(2,1)S(1)} collective-permute-done((bf16[2,4,1,9,128,128]{4,5,3,2,1,0:T(8,128)(2,1)S(1)}, bf16[2,4,1,9,128,128]{4,5,3,2,1,0:T(8,128)(2,1)S(1)}, u32[]{:S(2)}, u32[]{:S(2)}) %collective-permute-start.6) | collective-permute-done | bytes 2359328 | tf_op jit(solution)/shard_map/ppermute | solution.py:13
  140.4 1.9 %collective-permute-done.7 = bf16[2,4,1,9,128,128]{4,5,3,2,1,0:T(8,128)(2,1)S(1)} collective-permute-done((bf16[2,4,1,9,128,128]{4,5,3,2,1,0:T(8,128)(2,1)S(1)}, bf16[2,4,1,9,128,128]{4,5,3,2,1,0:T(8,128)(2,1)S(1)}, u32[]{:S(2)}, u32[]{:S(2)}) %collective-permute-start.7) | collective-permute-done | bytes 2359328 | tf_op jit(solution)/shard_map/ppermute | solution.py:16
  142.9 1.1 fusion.47
  144.3 1.4 add_dynamic-update-slice_fusion
  145.8 1.1 fusion.46
  146.8 2.1 %fusion.20 = f32[2,5,5,128,128]{3,4,2,1,0:T(8,128)S(1)} fusion(f32[2,5,5,128,128]{3,4,2,1,0:T(8,128)S(1)} %add_dynamic-update-slice_fusion, s32[]{:T(128)} %bitcast.50, s32[]{:T(128)} %bitcast.51, f32[2,3,3,128,128]{3,4,2,1,0:T(8,128)S(1)} %bitcast.314, pred[]{:T(512)} %and_reduce_fusion), kind=kLoop, calls=%fused_computation.30 | loop fusion | flops 589824 | bytes 3538953 | tf_op jit(solution)/shard_map/scatter-add | solution.py:89
  149.9 1.1 fusion.44
  151.6 1.1 fusion.43
  153.2 2.4 %copy.17 = bf16[2,5,5,128,128]{4,3,2,1,0:T(8,128)(2,1)} copy(bf16[2,5,5,128,128]{3,4,2,1,0:T(8,128)(2,1)S(1)} %convert_element_type.39) | data formatting | bytes 3276800 | tf_op jit(solution)/shard_map/convert_element_type | solution.py:90
  (65 shorter events, 14.1 us)
Async XLA Ops:
  1.1 6.4 %collective-permute-start = (bf16[1,2,4,128,128]{4,3,2,1,0:T(8,128)(2,1)S(1)}, bf16[1,2,4,128,128]{4,3,2,1,0:T(8,128)(2,1)S(1)}, u32[]{:S(2)}, u32[]{:S(2)}) collective-permute-start(bf16[1,2,4,128,128]{4,3,2,1,0:T(8,128)(2,1)S(1)} %get-tuple-element.148), channel_id=1, source_target_pairs={{0,32},{32,64},{64,96},{96,128},{128,160},{160,192},{192,224},{224... | collective-permute-start | bytes 786440 | tf_op jit(solution)/shard_map/ppermute | solution.py:13
  4.1 7.0 %collective-permute-start.1 = (bf16[1,2,4,128,128]{4,3,2,1,0:T(8,128)(2,1)S(1)}, bf16[1,2,4,128,128]{4,3,2,1,0:T(8,128)(2,1)S(1)}, u32[]{:S(2)}, u32[]{:S(2)}) collective-permute-start(bf16[1,2,4,128,128]{4,3,2,1,0:T(8,128)(2,1)S(1)} %get-tuple-element.147), channel_id=1, source_target_pairs={{32,0},{64,32},{96,64},{128,96},{160,128},{192,160},{224,192},{256... | collective-permute-start | bytes 786440 | tf_op jit(solution)/shard_map/ppermute | solution.py:16
  6.6 19.6 %copy-start.1 = (bf16[2,2,2,5,128,128]{5,4,3,2,1,0:T(8,128)(2,1)S(1)}, bf16[2,2,2,5,128,128]{5,4,3,2,1,0:T(8,128)(2,1)}, u32[]{:S(2)}) copy-start(bf16[2,2,2,5,128,128]{5,4,3,2,1,0:T(8,128)(2,1)} %param.22) | copy-start | bytes 3932164
  7.5 3.8 %copy-start.4 = (bf16[1,2,4,128,128]{4,3,2,1,0:T(8,128)(2,1)}, bf16[1,2,4,128,128]{4,3,2,1,0:T(8,128)(2,1)S(1)}, u32[]{:S(2)}) copy-start(bf16[1,2,4,128,128]{4,3,2,1,0:T(8,128)(2,1)S(1)} %collective-permute-done) | copy-start | bytes 786436
  11.2 15.2 %copy-start.5 = (bf16[1,2,4,128,128]{4,3,2,1,0:T(8,128)(2,1)}, bf16[1,2,4,128,128]{4,3,2,1,0:T(8,128)(2,1)S(1)}, u32[]{:S(2)}) copy-start(bf16[1,2,4,128,128]{4,3,2,1,0:T(8,128)(2,1)S(1)} %collective-permute-done.1) | copy-start | bytes 786436
  11.3 22.7 %collective-permute-start.3 = (bf16[4,1,4,128,128]{4,3,2,1,0:T(8,128)(2,1)S(1)}, bf16[4,1,4,128,128]{4,3,2,1,0:T(8,128)(2,1)S(1)}, u32[]{:S(2)}, u32[]{:S(2)}) collective-permute-start(bf16[4,1,4,128,128]{4,3,2,1,0:T(8,128)(2,1)S(1)} %get-tuple-element.138), channel_id=1, source_target_pairs={{1,0},{2,1},{3,2},{4,3},{5,4},{6,5},{7,6},{8,7},{9,8},{10,9},{11,1... | collective-permute-start | bytes 1572872 | tf_op jit(solution)/shard_map/ppermute | solution.py:16
  24.2 17.3 %collective-permute-start.2 = (bf16[4,1,4,128,128]{4,3,2,1,0:T(8,128)(2,1)S(1)}, bf16[4,1,4,128,128]{4,3,2,1,0:T(8,128)(2,1)S(1)}, u32[]{:S(2)}, u32[]{:S(2)}) collective-permute-start(bf16[4,1,4,128,128]{4,3,2,1,0:T(8,128)(2,1)S(1)} %get-tuple-element.137), channel_id=1, source_target_pairs={{0,1},{1,2},{2,3},{3,4},{4,5},{5,6},{6,7},{7,8},{8,9},{9,10},{10,1... | collective-permute-start | bytes 1572872 | tf_op jit(solution)/shard_map/ppermute | solution.py:13
  34.0 7.7 %copy-start.2 = (bf16[4,1,4,128,128]{4,3,2,1,0:T(8,128)(2,1)}, bf16[4,1,4,128,128]{4,3,2,1,0:T(8,128)(2,1)S(1)}, u32[]{:S(2)}) copy-start(bf16[4,1,4,128,128]{4,3,2,1,0:T(8,128)(2,1)S(1)} %collective-permute-done.3) | copy-start | bytes 1572868
  41.4 0.8 copy-start.3
  53.6 2.3 %copy-start = (bf16[20,4,128,128]{3,2,1,0:T(8,128)(2,1)S(1)}, bf16[20,4,128,128]{3,2,1,0:T(8,128)(2,1)}, u32[]{:S(2)}) copy-start(bf16[20,4,128,128]{3,2,1,0:T(8,128)(2,1)} %gather_fusion.1) | copy-start | bytes 7864324
  63.5 4.4 %copy-start.6 = (s32[5]{0:T(128)S(1)}, s32[5]{0:T(128)}, u32[]{:S(2)}) copy-start(s32[5]{0:T(128)} %constant.421.clone.1) | copy-start | bytes 64
  63.7 16.9 %collective-permute-start.5 = (bf16[2,1,2,9,128,128]{4,5,3,2,1,0:T(8,128)(2,1)S(1)}, bf16[2,1,2,9,128,128]{4,5,3,2,1,0:T(8,128)(2,1)S(1)}, u32[]{:S(2)}, u32[]{:S(2)}) collective-permute-start(bf16[2,1,2,9,128,128]{4,5,3,2,1,0:T(8,128)(2,1)S(1)} %get-tuple-element.132), channel_id=1, source_target_pairs={{32,0},{64,32},{96,64},{128,96},{160,128},{192,160},{224,192},{256... | collective-permute-start | bytes 3538952 | tf_op jit(solution)/shard_map/ppermute | solution.py:16
  63.8 16.8 %collective-permute-start.4 = (bf16[2,1,2,9,128,128]{4,5,3,2,1,0:T(8,128)(2,1)S(1)}, bf16[2,1,2,9,128,128]{4,5,3,2,1,0:T(8,128)(2,1)S(1)}, u32[]{:S(2)}, u32[]{:S(2)}) collective-permute-start(bf16[2,1,2,9,128,128]{4,5,3,2,1,0:T(8,128)(2,1)S(1)} %get-tuple-element.131), channel_id=1, source_target_pairs={{0,32},{32,64},{64,96},{96,128},{128,160},{160,192},{192,224},{224... | collective-permute-start | bytes 3538952 | tf_op jit(solution)/shard_map/ppermute | solution.py:13
  83.0 56.6 %collective-permute-start.6 = (bf16[2,4,1,9,128,128]{4,5,3,2,1,0:T(8,128)(2,1)S(1)}, bf16[2,4,1,9,128,128]{4,5,3,2,1,0:T(8,128)(2,1)S(1)}, u32[]{:S(2)}, u32[]{:S(2)}) collective-permute-start(bf16[2,4,1,9,128,128]{4,5,3,2,1,0:T(8,128)(2,1)S(1)} %get-tuple-element.122), channel_id=1, source_target_pairs={{0,1},{1,2},{2,3},{3,4},{4,5},{5,6},{6,7},{7,8},{8,9},{9,10},{10,1... | collective-permute-start | bytes 7077896 | tf_op jit(solution)/shard_map/ppermute | solution.py:13
  85.8 56.5 %collective-permute-start.7 = (bf16[2,4,1,9,128,128]{4,5,3,2,1,0:T(8,128)(2,1)S(1)}, bf16[2,4,1,9,128,128]{4,5,3,2,1,0:T(8,128)(2,1)S(1)}, u32[]{:S(2)}, u32[]{:S(2)}) collective-permute-start(bf16[2,4,1,9,128,128]{4,5,3,2,1,0:T(8,128)(2,1)S(1)} %get-tuple-element.121), channel_id=1, source_target_pairs={{1,0},{2,1},{3,2},{4,3},{5,4},{6,5},{7,6},{8,7},{9,8},{10,9},{11,1... | collective-permute-start | bytes 7077896 | tf_op jit(solution)/shard_map/ppermute | solution.py:16
where the time goes:
time: 157 us; the launch traced here: 156 us
  waiting for transfers between devices  73.6 us (47%)
  starting transfers between devices  29.6 us (19%)
  matrix products  23 us (15%)
  local copies, waits for them, and re-layouts  18.8 us (12%)
  other arithmetic  10.2 us (6%)
    ppermute x4, waiting for transfers between devices, padded(): lax.ppermute(lax.slice_in_dim(block, block.shape[dim] - width, None, axis...  49.8 us
    ppermute x4, waiting for transfers between devices, padded(): lax.ppermute(lax.slice_in_dim(block, 0, width, axis=dim), axis, backward)  23.9 us
    ppermute x4, starting transfers between devices, padded(): lax.ppermute(lax.slice_in_dim(block, 0, width, axis=dim), axis, backward)  19.8 us
    dot_general x2, matrix products, products_of_rows(): jnp.einsum('xykqj,xykqbc->xykjbc', onehot, picked, preferred_element_type...  11.5 us
    ppermute x4, starting transfers between devices, padded(): lax.ppermute(lax.slice_in_dim(block, block.shape[dim] - width, None, axis...  9.86 us
    dot_general x9, matrix products, assemble(): jnp.einsum('uab,sujac->sjbc', p_rows, w_rows, preferred_element_type=jnp....  6.83 us
    scatter-add x8, other arithmetic, assemble(): total.at[:, place[0]:place[0] + 3, place[1]:place[1] + 3].add(partial_terms)  5.38 us
    gather x2, local copies, waits for them, and re-layouts, products_of_rows(): picked = p_flat[position]  5.11 us
  transfers between devices with their start and end apart: 8, of which 7 were waited for; matrix products, arithmetic and copies ran while one was open for 8% of the time, Pallas kernels for 0%

commit v1 on v0

v1 whole, which is shorter than its diff:
```python
import jax
import jax.numpy as jnp
from jax import lax
from jax.experimental import pallas as pl
from jax.experimental.pallas import tpu as pltpu
from jax.sharding import PartitionSpec as P

MESH = pl.DeviceIdType.MESH
BF16 = jnp.bfloat16
F32 = jnp.float32

CORNER = {(-1, 0): 0, (-1, 1): 1, (0, 0): 1, (0, 1): 0, (1, 1): 0, (1, 2): 1}


def slot_table(a_off, a_count):
    slots = a_off.shape[-1]
    flip_x = jnp.array([1, -1], jnp.int32)[None, :, None, None]
    flip_y = jnp.array([1, -1], jnp.int32)[None, None, :, None]
    place = (flip_x * (a_off // 3 - 1) + 1) * 3 + flip_y * (a_off % 3 - 1) + 1
    number = jnp.arange(slots, dtype=jnp.int32)
    hit = (place[..., None] == jnp.arange(9, dtype=jnp.int32)) & (number < a_count[..., None])[..., None]
    table = jnp.min(jnp.where(hit, number[:, None], slots), axis=3)
    operators, rows, cols = table.shape[:3]
    table = jnp.moveaxis(table, 2, 0).reshape(cols, operators * rows, 9)
    return jnp.pad(table, ((0, 0), (0, 8 - operators * rows), (0, 128 - 9)))


def kernel(row_count, col_count, a_hbm, p_hbm, t_hbm, out_ref,
           p_win, a_own, a_one, a_two, slot_of, w_buf, lhs_t, own, prod, recv,
           local_sem, col_send, col_recv, row_send, row_recv, prod_send, prod_recv):
    r = lax.axis_index("row")
    c = lax.axis_index("col")
    rows = [lax.rem(r + row_count - 1, row_count), lax.rem(r + 1, row_count)]
    cols = [lax.rem(c + col_count - 1, col_count), lax.rem(c + 1, col_count)]
    first = lax.rem(r, 2)
    second = 1 - first
    size = p_hbm.shape[-1]

    def to_row(number):
        return {"row": lax.rem(r + 2 * number - 1 + row_count, row_count), "col": c}

    barrier = pltpu.get_barrier_semaphore()
    for side in range(2):
        pl.semaphore_signal(barrier, inc=1, device_id={"row": rows[side], "col": c}, device_id_type=MESH)
        pl.semaphore_signal(barrier, inc=1, device_id={"row": r, "col": cols[side]}, device_id_type=MESH)

    local = [
        pltpu.make_async_copy(p_hbm, p_win.at[1:3, 2:4], local_sem.at[0]),
        pltpu.make_async_copy(a_hbm, a_own.at[:, :, :, 0:5], local_sem.at[1]),
        pltpu.make_async_copy(t_hbm, slot_of.at[1:3], local_sem.at[2]),
    ]
    for copy in local:
        copy.start()
    pl.semaphore_wait(barrier, 4)

    def remote(src, dst, send, recv_s, device):
        return pltpu.make_async_remote_copy(
            src_ref=src, dst_ref=dst, send_sem=send, recv_sem=recv_s,
            device_id=device, device_id_type=MESH,
        )

    col_copies = [[], []]
    for side in range(2):
        device = {"row": r, "col": cols[side]}
        land = 1 - side
        near, far = side, 1 - side
        near_at = 1 if land == 0 else 4
        far_at = 0 if land == 0 else 5
        table_at = 0 if land == 0 else 3
        parts = [
            (t_hbm.at[near], slot_of.at[table_at]),
            (p_hbm.at[:, near], p_win.at[1:3, near_at]),
            (p_hbm.at[:, far], p_win.at[1:3, far_at]),
            (a_hbm.at[:, first, near], a_one.at[land, :, 0:5]),
            (a_hbm.at[:, second, near], a_two.at[land, :, 0:5]),
        ]
        for number, (src, dst) in enumerate(parts):
            col_copies[side].append(
                remote(src, dst, col_send.at[side, number], col_recv.at[land, number], device)
            )
    row_copies = [[], []]
    for number in range(2):
        device = to_row(number)
        row_at = 3 if number == 0 else 0
        parts = [(p_hbm.at[number], p_win.at[row_at, 2:4])]
        for at in (1, 4, 0, 5):
            parts.append((p_win.at[1 + number, at], p_win.at[row_at, at]))
        for part, (src, dst) in enumerate(parts):
            row_copies[number].append(
                remote(src, dst, row_send.at[number, part], row_recv.at[number, part], device)
            )

    for part in range(5):
        for side in range(2):
            col_copies[side][part].start()
        if part == 0:
            for number in range(2):
                row_copies[number][0].start()

    zero = jnp.zeros((size, size), BF16)
    for operator in range(2):
        for side in range(2):
            a_one[side, operator, 5] = zero
            a_two[side, operator, 5] = zero
            for number in range(2):
                a_own[operator, number, side, 5] = zero

    def wait_col(part):
        for side in range(2):
            col_copies[side][part].wait_recv()

    def wait_row(part):
        for number in range(2):
            row_copies[number][part].wait_recv()

    def fine_rows(number, column, load):
        flip_x = 1 - 2 * number
        flip_y = 2 * lax.rem(column, 2) - 1

        def p_block(off_x, off_y, corner_x, corner_y):
            return p_win[number + 1 + flip_x * off_x, column + 1 + flip_y * off_y, 2 * corner_x + corner_y]

        for place_x in range(3):
            offs_x = [off for off in (-1, 0, 1) if (off, place_x) in CORNER]
            results = []
            for offs_y, places_y in (((-1, 0), (0, 1)), ((1,), (1, 2))):
                pairs = [(off_x, off_y) for off_x in offs_x for off_y in offs_y]
                left = jnp.concatenate(
                    [
                        jnp.concatenate(
                            [load(operator, (off_x + 1) * 3 + off_y + 1) for operator in range(2)], axis=0
                        )
                        for off_x, off_y in pairs
                    ],
                    axis=1,
                )
                right = jnp.concatenate(
                    [
                        jnp.concatenate(
                            [
                                p_block(off_x, off_y, CORNER[off_x, place_x], CORNER[off_y, place_y])
                                for place_y in places_y
                            ],
                            axis=1,
                        )
                        for off_x, off_y in pairs
                    ],
                    axis=0,
                )
                results.append(jnp.dot(left, right, preferred_element_type=F32))
            low, high = results
            columns = [low[:, :size], low[:, size:] + high[:, :size], high[:, size:]]
            for place_y in range(3):
                for operator in range(2):
                    w_buf[number, column, 1 + flip_x * (place_x - 1), 1 + flip_y * (place_y - 1), operator] = (
                        columns[place_y][operator * size : (operator + 1) * size].astype(BF16)
                    )

    def transposes(number, columns):
        for column in columns:
            corner_y = 1 if column in (0, 3) else 0
            for corner_x in range(2):
                lhs_t[number, corner_x * size : (corner_x + 1) * size, column * size : (column + 1) * size] = p_win[
                    1 + number, column + 1, 2 * corner_x + corner_y
                ].T

    def products(number, place_x, start):
        for place_n in range(5):
            low = [0, 0, 0, 1, 3][place_n]
            high = [1, 3, 4, 4, 4][place_n]
            right = jnp.concatenate(
                [
                    jnp.concatenate(
                        [
                            w_buf[number, column, place_x, place_n - [0, 1, 1, 2][column], operator]
                            for operator in range(2)
                        ],
                        axis=1,
                    )
                    for column in range(low, high)
                ],
                axis=0,
            )
            left = lhs_t[number, :, low * size : high * size]
            result = jnp.dot(left, right, preferred_element_type=F32)
            for operator in range(2):
                lanes = slice(operator * size, (operator + 1) * size)
                if start:
                    own[place_x, place_n, operator] = result[:size, lanes]
                else:
                    own[place_x, place_n, operator] += result[:size, lanes]
                prod[number, place_x, place_n, operator] = result[size:, lanes].astype(BF16)

    def halo_row(number, halo):
        @pl.loop(0, 2)
        def _(side):
            def load(operator, place):
                return halo[side, operator, slot_of[3 * side, operator * 2 + number, place]]

            fine_rows(number, 3 * side, load)

    wait_col(1)
    for number in range(2):
        row_copies[number][1].start()
        row_copies[number][2].start()
    for copy in local:
        copy.wait()
    for number in range(2):
        transposes(number, range(4))
    wait_row(0)
    wait_row(1)
    wait_row(2)

    @pl.loop(0, 4)
    def _(step):
        number = step // 2
        column = lax.rem(step, 2)

        def load(operator, place):
            return a_own[operator, number, column, slot_of[1 + column, operator * 2 + number, place]]

        fine_rows(number, 1 + column, load)

    wait_col(2)
    for number in range(2):
        row_copies[number][3].start()
        row_copies[number][4].start()
    wait_col(0)
    wait_col(3)
    wait_row(3)
    wait_row(4)

    prod_copies = []

    def send(number, order):
        def at(place_x):
            copy = remote(
                prod.at[number, place_x], recv.at[number, place_x],
                prod_send.at[order, place_x], prod_recv.at[number, place_x], to_row(number),
            )
            copy.start()
            prod_copies.append(copy)
        return at

    for order, (number, halo) in enumerate(((first, a_one), (second, a_two))):
        if order == 1:
            wait_col(4)
        halo_row(number, halo)
        push = send(number, order)
        for place_x in range(3):
            products(number, place_x, order == 0)
            push(place_x)

    for copy in prod_copies:
        copy.wait_recv()

    @pl.loop(0, 5)
    def _(place_n):
        for operator in range(2):
            for place in range(5):
                total = None
                if 1 <= place <= 3:
                    total = own[place - 1, place_n, operator]
                if place >= 2:
                    term = recv[0, place - 2, place_n, operator].astype(F32)
                    total = term if total is None else total + term
                if place <= 2:
                    term = recv[1, place, place_n, operator].astype(F32)
                    total = term if total is None else total + term
                out_ref[operator, place, place_n] = total.astype(BF16)

    for copies in col_copies + row_copies + [prod_copies]:
        for copy in copies:
            copy.wait_send()


def per_device(a_vals, a_off, a_count, p_vals):
    operators, size = a_vals.shape[0], a_vals.shape[-1]
    table = slot_table(a_off, a_count)
    rows, cols = lax.axis_size("row"), lax.axis_size("col")

    def body(*refs):
        kernel(rows, cols, *refs)

    block = (size, size)
    result = pl.pallas_call(
        body,
        out_shape=jax.ShapeDtypeStruct((operators, 5, 5) + block, BF16),
        in_specs=[pl.BlockSpec(memory_space=pl.ANY)] * 3,
        out_specs=pl.BlockSpec(memory_space=pltpu.VMEM),
        scratch_shapes=[
            pltpu.VMEM((4, 6, 4) + block, BF16),
            pltpu.VMEM((2, 2, 2, 6) + block, BF16),
            pltpu.VMEM((2, 2, 6) + block, BF16),
            pltpu.VMEM((2, 2, 6) + block, BF16),
            pltpu.SMEM((4, 8, 128), jnp.int32),
            pltpu.VMEM((2, 4, 3, 3, 2) + block, BF16),
            pltpu.VMEM((2, 2 * size, 4 * size), BF16),
            pltpu.VMEM((3, 5, 2) + block, F32),
            pltpu.VMEM((2, 3, 5, 2) + block, BF16),
            pltpu.VMEM((2, 3, 5, 2) + block, BF16),
            pltpu.SemaphoreType.DMA((3,)),
            pltpu.SemaphoreType.DMA((2, 5)),
            pltpu.SemaphoreType.DMA((2, 5)),
            pltpu.SemaphoreType.DMA((2, 5)),
            pltpu.SemaphoreType.DMA((2, 5)),
            pltpu.SemaphoreType.DMA((2, 3)),
            pltpu.SemaphoreType.DMA((2, 3)),
        ],
        compiler_params=pltpu.CompilerParams(
            collective_id=0, has_side_effects=True, vmem_limit_bytes=48 * 1024 * 1024
        ),
        name="galerkin",
    )(a_vals, p_vals, table)
    return result.reshape((operators, 1, 1, 25) + block)


def solution(mesh):
    placed = (
        P(None, "row", "col", None, None, None),
        P(None, "row", "col", None),
        P(None, "row", "col"),
        P("row", "col", None, None, None),
    )
    return jax.shard_map(
        per_device,
        mesh=mesh,
        in_specs=placed,
        out_specs=P(None, "row", "col", None, None, None),
        check_vma=False,
    )
```

time: 157 us -> 56.2 us (0.36)
  waiting for transfers between devices: 73.6 us -> 0 us
  Pallas kernels: 0 us -> 50.6 us
  starting transfers between devices: 29.6 us -> 0 us
  matrix products: 23 us -> 0 us
  local copies, waits for them, and re-layouts: 18.8 us -> 3.64 us
  other arithmetic: 10.2 us -> 1.61 us
    ppermute x8 -> x0, waiting for transfers between devices: 73.6 us -> none  [the longest x4 49.8 us: padded(): lax.ppermute(lax.slice_in_dim(block, block.shape[dim] - width, None, axis...]
    pallas_call x0 -> x1, Pallas kernels: none -> 50.6 us  [per_device(): pl.pallas_call(body, out_shape=jax.ShapeDtypeStruct((operators, 5, 5) + b...]
    ppermute x8 -> x0, starting transfers between devices: 29.6 us -> none  [the longest x4 19.8 us: padded(): lax.ppermute(lax.slice_in_dim(block, 0, width, axis=dim), axis, backward)]
    dot_general x13 -> x0, matrix products: 23 us -> none  [the longest x2 11.5 us: products_of_rows(): jnp.einsum('xykqj,xykqbc->xykjbc', onehot, picked, preferred_element_type...]
    another operation x12 -> x0, local copies, waits for them, and re-layouts: 5.56 us -> none  [the longest x5 3.95 us: assemble(): jnp.stack([p_window[lag_x + p_margin, lag_y + p_margin, quadrant] for lag...]
    scatter-add x8 -> x0, other arithmetic: 5.38 us -> none  [assemble(): total.at[:, place[0]:place[0] + 3, place[1]:place[1] + 3].add(partial_terms)]
    gather x2 -> x0, local copies, waits for them, and re-layouts: 5.11 us -> none  [products_of_rows(): picked = p_flat[position]]
    slice x3 -> x0, local copies, waits for them, and re-layouts: 2.96 us -> none  [the longest x2 2.89 us: padded(): lax.slice_in_dim(block, 0, width, axis=dim)]
  transfers between devices with their start and end apart: 8 -> 0, of which waited for: 7 -> 0; matrix products, arithmetic and copies ran while one was open for 8% -> 0% of each run, Pallas kernels for 0% -> 0%
where the time goes in v1:
time: 56.2 us; the launch traced here: 55.9 us
  Pallas kernels  50.6 us (90%)
  local copies, waits for them, and re-layouts  3.64 us (6%)
  other arithmetic  1.61 us (3%)
    pallas_call x1, Pallas kernels, per_device(): pl.pallas_call(body, out_shape=jax.ShapeDtypeStruct((operators, 5, 5) + b...  50.6 us
    unnamed x5, local copies, waits for them, and re-layouts  3.52 us

profile of v1, /device:TPU:25, one launch (start us, length us, event | category | flops | bytes accessed | tf_op | source)
XLA Modules:
  0.0 55.9 jit_solution(8405479470328095504)
XLA Ops:
  0.0 0.8 %add_add_fusion = s32[2,2,2,5]{3,2,1,0:T(2,128)S(1)} fusion(s32[2,2,2,5]{3,2,1,0:T(2,128)} %param.7, s32[2]{0:T(128)} %constant.31.clone), kind=kLoop, calls=%fused_computation.6 | loop fusion | flops 800 | bytes 328 | tf_op jit(solution)/shard_map/add | solution.py:19
  0.8 0.7 %iota_compare_fusion = pred[2,2,2,5]{2,3,1,0:T(8,128)(4,1)S(1)} fusion(s32[2,2,2]{2,1,0:T(2,128)} %param.8), kind=kLoop, calls=%fused_computation.2 | loop fusion | flops 40 | bytes 72 | tf_op jit(solution)/shard_map/lt | solution.py:21
  1.5 0.1 copy.8
  1.6 0.1 fusion
  1.8 0.0 copy-start
  1.8 1.3 %copy-done = bf16[2,2,2,5,128,128]{5,4,3,2,1,0:T(8,128)(2,1)S(1)} copy-done((bf16[2,2,2,5,128,128]{5,4,3,2,1,0:T(8,128)(2,1)S(1)}, bf16[2,2,2,5,128,128]{5,4,3,2,1,0:T(8,128)(2,1)}, u32[]{:S(2)}) %copy-start) | copy-done | bytes 1310744
  3.1 0.0 copy-start.1
  3.1 1.0 %copy-done.1 = bf16[2,2,4,128,128]{4,3,2,1,0:T(8,128)(2,1)S(1)} copy-done((bf16[2,2,4,128,128]{4,3,2,1,0:T(8,128)(2,1)S(1)}, bf16[2,2,4,128,128]{4,3,2,1,0:T(8,128)(2,1)}, u32[]{:S(2)}) %copy-start.1) | copy-done | bytes 524312
  4.1 50.6 %galerkin.1 = bf16[2,5,5,128,128]{4,3,2,1,0:T(8,128)(2,1)S(1)} custom-call(bf16[2,2,2,5,128,128]{5,4,3,2,1,0:T(8,128)(2,1)S(1)} %copy-done, bf16[2,2,4,128,128]{4,3,2,1,0:T(8,128)(2,1)S(1)} %copy-done.1, s32[2,8,128]{2,1,0:T(8,128)S(1)} %pad.4.refs_2_), custom_call_target="tpu_custom_call" | custom-call | tf_op jit(solution)/shard_map/galerkin/pallas_call | solution.py:286
  54.8 1.2 %copy.12 = bf16[2,1,1,25,128,128]{5,4,3,2,1,0:T(8,128)(2,1)} copy(bf16[2,1,1,25,128,128]{5,4,3,2,1,0:T(8,128)(2,1)S(1)} %bitcast.5) | data formatting | bytes 3276800
  (2 shorter events, 0.0 us)
Async XLA Ops:
  1.8 1.3 %copy-start = (bf16[2,2,2,5,128,128]{5,4,3,2,1,0:T(8,128)(2,1)S(1)}, bf16[2,2,2,5,128,128]{5,4,3,2,1,0:T(8,128)(2,1)}, u32[]{:S(2)}) copy-start(bf16[2,2,2,5,128,128]{5,4,3,2,1,0:T(8,128)(2,1)} %refs_0_.1) | copy-start | bytes 3932164
  3.1 1.0 %copy-start.1 = (bf16[2,2,4,128,128]{4,3,2,1,0:T(8,128)(2,1)S(1)}, bf16[2,2,4,128,128]{4,3,2,1,0:T(8,128)(2,1)}, u32[]{:S(2)}) copy-start(bf16[2,2,4,128,128]{4,3,2,1,0:T(8,128)(2,1)} %refs_1_.1) | copy-start | bytes 1572868

commit v2 on v1

v2 whole, which is shorter than its diff:
```python
import jax
import jax.numpy as jnp
from jax import lax
from jax.experimental import pallas as pl
from jax.experimental.pallas import tpu as pltpu
from jax.sharding import PartitionSpec as P

MESH = pl.DeviceIdType.MESH
BF16 = jnp.bfloat16
F32 = jnp.float32

CORNER = {(-1, 0): 0, (-1, 1): 1, (0, 0): 1, (0, 1): 0, (1, 1): 0, (1, 2): 1}


def kernel(row_count, col_count, a_hbm, p_hbm, off_hbm, count_hbm, out_ref,
           p_win, a_own, a_half_0, a_half_1, a_half_2, a_half_3,
           off_ref, count_ref, off_halo, count_halo, slot_of,
           w_buf, lhs_t, own, prod, recv,
           local_sem, col_send, col_recv, row_send, row_recv, prod_send, prod_recv):
    r = lax.axis_index("row")
    c = lax.axis_index("col")
    rows = [lax.rem(r + row_count - 1, row_count), lax.rem(r + 1, row_count)]
    cols = [lax.rem(c + col_count - 1, col_count), lax.rem(c + 1, col_count)]
    first = lax.rem(r, 2)
    order = (first, 1 - first)
    halves = ((a_half_0, a_half_1), (a_half_2, a_half_3))
    size = p_hbm.shape[-1]
    slots = a_hbm.shape[3]

    def to_row(number):
        return {"row": lax.rem(r + 2 * number - 1 + row_count, row_count), "col": c}

    barrier = pltpu.get_barrier_semaphore()
    for side in range(2):
        pl.semaphore_signal(barrier, inc=1, device_id={"row": rows[side], "col": c}, device_id_type=MESH)
        pl.semaphore_signal(barrier, inc=1, device_id={"row": r, "col": cols[side]}, device_id_type=MESH)

    local = [
        pltpu.make_async_copy(p_hbm, p_win.at[1:3, 2:4], local_sem.at[0]),
        pltpu.make_async_copy(a_hbm, a_own.at[:, :, :, 0:slots], local_sem.at[1]),
        pltpu.make_async_copy(off_hbm, off_ref, local_sem.at[2]),
        pltpu.make_async_copy(count_hbm, count_ref, local_sem.at[3]),
    ]
    for copy in local:
        copy.start()
    pl.semaphore_wait(barrier, 4)

    def remote(src, dst, send, recv_s, device):
        return pltpu.make_async_remote_copy(
            src_ref=src, dst_ref=dst, send_sem=send, recv_sem=recv_s,
            device_id=device, device_id_type=MESH,
        )

    col_copies = [[], []]
    for side in range(2):
        device = {"row": r, "col": cols[side]}
        land = 1 - side
        near = side
        at = 0 if land == 0 else 4
        parts = [(p_hbm.at[number], p_win.at[1 + number, at : at + 2]) for number in order]
        for turn in range(2):
            for operator in range(2):
                parts.append(
                    (a_hbm.at[operator, order[turn], near], halves[turn][operator].at[land, 0:slots])
                )
        parts.append((off_hbm, off_halo.at[land]))
        parts.append((count_hbm, count_halo.at[land]))
        for part, (src, dst) in enumerate(parts):
            col_copies[side].append(
                remote(src, dst, col_send.at[side, part], col_recv.at[land, part], device)
            )
    row_copies = [[], []]
    for turn in range(2):
        number = order[turn]
        row_at = 3 * (1 - number)
        parts = [(p_hbm.at[number], p_win.at[row_at, 2:4])]
        for at in (0, 4):
            parts.append((p_win.at[1 + number, at : at + 2], p_win.at[row_at, at : at + 2]))
        for part, (src, dst) in enumerate(parts):
            row_copies[turn].append(
                remote(src, dst, row_send.at[turn, part], row_recv.at[number, part], to_row(number))
            )

    def start_col(part):
        for side in range(2):
            col_copies[side][part].start()

    def wait_col(part):
        for side in range(2):
            col_copies[side][part].wait_recv()

    for part in (6, 7, 0):
        start_col(part)
    for turn in range(2):
        row_copies[turn][0].start()
    for part in (1, 2, 3, 4, 5):
        start_col(part)

    zero = jnp.zeros((size, size), BF16)
    for operator in range(2):
        for side in range(2):
            for turn in range(2):
                halves[turn][operator][side, slots] = zero
                a_own[operator, turn, side, slots] = zero

    def table(column, off_at, count_at):
        @pl.loop(0, 4)
        def _(line):
            operator = line // 2
            number = lax.rem(line, 2)
            flip_x = 1 - 2 * number
            flip_y = 2 * (column % 2) - 1
            count = count_at(operator, number)
            places = []
            for slot in range(slots):
                off = off_at(operator, number, slot)
                off_x = (off >= 3).astype(jnp.int32) + (off >= 6).astype(jnp.int32)
                off_y = off - 3 * off_x
                place = 3 * (flip_x * (off_x - 1) + 1) + flip_y * (off_y - 1) + 1
                places.append(jnp.where(slot < count, place, -1))
            for position in range(9):
                found = jnp.int32(slots)
                for slot in range(slots):
                    found = jnp.where(places[slot] == position, slot, found)
                slot_of[column, line, position] = found

    def halo_table(side):
        table(
            3 * side,
            lambda operator, number, slot: off_halo[side, operator, number, 1 - side, slot],
            lambda operator, number: count_halo[side, operator, number, 1 - side],
        )

    def fine_rows(number, column, operators, load):
        flip_x = 1 - 2 * number
        flip_y = 2 * lax.rem(column, 2) - 1

        def p_block(off_x, off_y, corner_x, corner_y):
            return p_win[number + 1 + flip_x * off_x, column + 1 + flip_y * off_y, 2 * corner_x + corner_y]

        for place_x in range(3):
            offs_x = [off for off in (-1, 0, 1) if (off, place_x) in CORNER]
            results = []
            for offs_y, places_y in (((-1, 0), (0, 1)), ((1,), (1, 2))):
                pairs = [(off_x, off_y) for off_x in offs_x for off_y in offs_y]
                left = jnp.concatenate(
                    [
                        jnp.concatenate(
                            [load(operator, (off_x + 1) * 3 + off_y + 1) for operator in operators], axis=0
                        )
                        for off_x, off_y in pairs
                    ],
                    axis=1,
                )
                right = jnp.concatenate(
                    [
                        jnp.concatenate(
                            [
                                p_block(off_x, off_y, CORNER[off_x, place_x], CORNER[off_y, place_y])
                                for place_y in places_y
                            ],
                            axis=1,
                        )
                        for off_x, off_y in pairs
                    ],
                    axis=0,
                )
                results.append(jnp.dot(left, right, preferred_element_type=F32))
            low, high = results
            columns = [low[:, :size], low[:, size:] + high[:, :size], high[:, size:]]
            for place_y in range(3):
                for at, operator in enumerate(operators):
                    w_buf[operator, number, column, 1 + flip_x * (place_x - 1), 1 + flip_y * (place_y - 1)] = (
                        columns[place_y][at * size : (at + 1) * size].astype(BF16)
                    )

    def transposes(number):
        for column in range(4):
            corner_y = 1 if column in (0, 3) else 0
            for corner_x in range(2):
                lhs_t[number, corner_x * size : (corner_x + 1) * size, column * size : (column + 1) * size] = p_win[
                    1 + number, column + 1, 2 * corner_x + corner_y
                ].T

    def products(operator, number, places, start):
        for place_n in range(5):
            low = [0, 0, 0, 1, 3][place_n]
            high = [1, 3, 4, 4, 4][place_n]
            right = jnp.concatenate(
                [
                    jnp.concatenate(
                        [
                            w_buf[operator, number, column, place_x, place_n - [0, 1, 1, 2][column]]
                            for place_x in places
                        ],
                        axis=1,
                    )
                    for column in range(low, high)
                ],
                axis=0,
            )
            left = lhs_t[number, :, low * size : high * size]
            result = jnp.dot(left, right, preferred_element_type=F32)
            for at, place_x in enumerate(places):
                lanes = slice(at * size, (at + 1) * size)
                if start:
                    own[operator, place_x, place_n] = result[:size, lanes]
                else:
                    own[operator, place_x, place_n] += result[:size, lanes]
                prod[operator, number, place_x, place_n] = result[size:, lanes].astype(BF16)

    def own_row(number):
        @pl.loop(0, 2)
        def _(column):
            def load(operator, place):
                return a_own[operator, number, column, slot_of[1 + column, operator * 2 + number, place]]

            fine_rows(number, 1 + column, (0, 1), load)

    for copy in local:
        copy.wait()
    for column in (1, 2):
        table(
            column,
            lambda operator, number, slot, column=column: off_ref[operator, number, column - 1, slot],
            lambda operator, number, column=column: count_ref[operator, number, column - 1],
        )
    wait_col(6)
    wait_col(7)
    for side in range(2):
        halo_table(side)
    for turn in range(2):
        wait_col(turn)
        for part in (1, 2):
            row_copies[turn][part].start()
        transposes(order[turn])
    for copies in row_copies:
        for copy in copies:
            copy.wait_recv()

    prod_copies = [[], []]
    for turn in range(2):
        number = order[turn]
        own_row(number)
        for operator in range(2):
            half = halves[turn][operator]
            wait_col(2 + 2 * turn + operator)

            @pl.loop(0, 2)
            def _(side):
                def load(operator, place):
                    return half[side, slot_of[3 * side, operator * 2 + number, place]]

                fine_rows(number, 3 * side, (operator,), load)

            for piece, places in enumerate(((0, 1), (2,))):
                products(operator, number, places, turn == 0)
                part = slice(places[0], places[-1] + 1)
                copy = remote(
                    prod.at[operator, number, part], recv.at[operator, number, part],
                    prod_send.at[operator, turn, piece], prod_recv.at[operator, number, piece], to_row(number),
                )
                copy.start()
                prod_copies[operator].append(copy)

    for operator in range(2):
        for copy in prod_copies[operator]:
            copy.wait_recv()

        @pl.loop(0, 5)
        def _(place_n):
            for place in range(5):
                total = None
                if 1 <= place <= 3:
                    total = own[operator, place - 1, place_n]
                if place >= 2:
                    term = recv[operator, 0, place - 2, place_n].astype(F32)
                    total = term if total is None else total + term
                if place <= 2:
                    term = recv[operator, 1, place, place_n].astype(F32)
                    total = term if total is None else total + term
                out_ref[operator, place, place_n] = total.astype(BF16)

    for copies in col_copies + row_copies + prod_copies:
        for copy in copies:
            copy.wait_send()


def per_device(a_vals, a_off, a_count, p_vals):
    operators, size = a_vals.shape[0], a_vals.shape[-1]
    slots = a_vals.shape[3]
    rows, cols = lax.axis_size("row"), lax.axis_size("col")

    def body(*refs):
        kernel(rows, cols, *refs)

    block = (size, size)
    in_hbm = pl.BlockSpec(memory_space=pl.ANY)
    result = pl.pallas_call(
        body,
        out_shape=jax.ShapeDtypeStruct((operators, 5, 5) + block, BF16),
        in_specs=[in_hbm] * 4,
        out_specs=pl.BlockSpec(memory_space=pltpu.VMEM),
        scratch_shapes=[
            pltpu.VMEM((4, 6, 4) + block, BF16),
            pltpu.VMEM((2, 2, 2, slots + 1) + block, BF16),
        ]
        + [pltpu.VMEM((2, slots + 1) + block, BF16)] * 4
        + [
            pltpu.SMEM(a_off.shape, jnp.int32),
            pltpu.SMEM(a_count.shape, jnp.int32),
            pltpu.SMEM((2,) + a_off.shape, jnp.int32),
            pltpu.SMEM((2,) + a_count.shape, jnp.int32),
            pltpu.SMEM((4, 8, 128), jnp.int32),
            pltpu.VMEM((2, 2, 4, 3, 3) + block, BF16),
            pltpu.VMEM((2, 2 * size, 4 * size), BF16),
            pltpu.VMEM((2, 3, 5) + block, F32),
            pltpu.VMEM((2, 2, 3, 5) + block, BF16),
            pltpu.VMEM((2, 2, 3, 5) + block, BF16),
            pltpu.SemaphoreType.DMA((4,)),
            pltpu.SemaphoreType.DMA((2, 8)),
            pltpu.SemaphoreType.DMA((2, 8)),
            pltpu.SemaphoreType.DMA((2, 3)),
            pltpu.SemaphoreType.DMA((2, 3)),
            pltpu.SemaphoreType.DMA((2, 2, 2)),
            pltpu.SemaphoreType.DMA((2, 2, 2)),
        ],
        compiler_params=pltpu.CompilerParams(
            collective_id=0, has_side_effects=True, vmem_limit_bytes=48 * 1024 * 1024
        ),
        name="galerkin",
    )(*[pltpu.with_memory_space_constraint(array, pltpu.HBM) for array in (a_vals, p_vals, a_off, a_count)])
    return result.reshape((operators, 1, 1, 25) + block)


def solution(mesh):
    placed = (
        P(None, "row", "col", None, None, None),
        P(None, "row", "col", None),
        P(None, "row", "col"),
        P("row", "col", None, None, None),
    )
    return jax.shard_map(
        per_device,
        mesh=mesh,
        in_specs=placed,
        out_specs=P(None, "row", "col", None, None, None),
        check_vma=False,
    )
```

time: 56.2 us -> 47.9 us (0.85)
  Pallas kernels: 50.6 us -> 46.6 us
  local copies, waits for them, and re-layouts: 3.64 us -> 1.17 us
  other arithmetic: 1.61 us -> 0 us
    pallas_call x1, Pallas kernels: 50.6 us -> 46.6 us  [per_device(): pl.pallas_call(body, out_shape=jax.ShapeDtypeStruct((operators, 5, 5) + b...]
    unnamed x5 -> x1, local copies, waits for them, and re-layouts: 3.52 us -> 1.17 us
    add x1 -> x0, other arithmetic: 0.81 us -> none  [slot_table(): place = (flip_x * (a_off // 3 - 1) + 1) * 3 + flip_y * (a_off % 3 - 1) + 1]
    lt x1 -> x0, other arithmetic: 0.69 us -> none  [slot_table(): number < a_count[..., None]]
where the time goes in v2:
time: 47.9 us; the launch traced here: 47.8 us
  Pallas kernels  46.6 us (97%)
  local copies, waits for them, and re-layouts  1.17 us (2%)
    pallas_call x1, Pallas kernels, per_device(): pl.pallas_call(body, out_shape=jax.ShapeDtypeStruct((operators, 5, 5) + b...  46.6 us
    unnamed x1, local copies, waits for them, and re-layouts  1.17 us

profile of v2, /device:TPU:25, one launch (start us, length us, event | category | flops | bytes accessed | tf_op | source)
XLA Modules:
  0.0 47.8 jit_solution(11216253424675764612)
XLA Ops:
  0.0 46.6 %galerkin.1 = bf16[2,5,5,128,128]{4,3,2,1,0:T(8,128)(2,1)S(1)} custom-call(bf16[2,2,2,5,128,128]{5,4,3,2,1,0:T(8,128)(2,1)} %refs_0_.1, bf16[2,2,4,128,128]{4,3,2,1,0:T(8,128)(2,1)} %refs_1_.1, s32[2,2,2,5]{3,2,1,0:T(2,128)} %refs_2_.1, s32[2,2,2]{2,1,0:T(2,128)} %refs_3_.1), custom_call_target="tpu_custom_call" | custom-call | tf_op jit(solution)/shard_map/galerkin/pallas_call | solution.py:299
  46.6 1.2 %copy.7 = bf16[2,1,1,25,128,128]{5,4,3,2,1,0:T(8,128)(2,1)} copy(bf16[2,1,1,25,128,128]{5,4,3,2,1,0:T(8,128)(2,1)S(1)} %bitcast.3) | data formatting | bytes 3276800

commit v3 on v2

--- a/solution.py
+++ b/solution.py
@@ -13,7 +13,7 @@
 
 
 def kernel(row_count, col_count, a_hbm, p_hbm, off_hbm, count_hbm, out_ref,
-           p_win, a_own, a_half_0, a_half_1, a_half_2, a_half_3,
+           p_win, a_own, a_0, a_1, a_2, a_3, a_4, a_5, a_6, a_7,
            off_ref, count_ref, off_halo, count_halo, slot_of,
            w_buf, lhs_t, own, prod, recv,
            local_sem, col_send, col_recv, row_send, row_recv, prod_send, prod_recv):
@@ -23,7 +23,7 @@
     cols = [lax.rem(c + col_count - 1, col_count), lax.rem(c + 1, col_count)]
     first = lax.rem(r, 2)
     order = (first, 1 - first)
-    halves = ((a_half_0, a_half_1), (a_half_2, a_half_3))
+    halves = (((a_0, a_1), (a_2, a_3)), ((a_4, a_5), (a_6, a_7)))
     size = p_hbm.shape[-1]
     slots = a_hbm.shape[3]
 
@@ -61,7 +61,7 @@
         for turn in range(2):
             for operator in range(2):
                 parts.append(
-                    (a_hbm.at[operator, order[turn], near], halves[turn][operator].at[land, 0:slots])
+                    (a_hbm.at[operator, order[turn], near], halves[turn][operator][land].at[0:slots])
                 )
         parts.append((off_hbm, off_halo.at[land]))
         parts.append((count_hbm, count_halo.at[land]))
@@ -85,22 +85,21 @@
         for side in range(2):
             col_copies[side][part].start()
 
-    def wait_col(part):
-        for side in range(2):
-            col_copies[side][part].wait_recv()
-
-    for part in (6, 7, 0):
-        start_col(part)
+    def wait_col(part, sides=(0, 1)):
+        for side in sides:
+            col_copies[1 - side][part].wait_recv()
+
+    start_col(0)
     for turn in range(2):
         row_copies[turn][0].start()
-    for part in (1, 2, 3, 4, 5):
+    for part in (6, 7, 1, 2, 3, 4, 5):
         start_col(part)
 
     zero = jnp.zeros((size, size), BF16)
     for operator in range(2):
         for side in range(2):
             for turn in range(2):
-                halves[turn][operator][side, slots] = zero
+                halves[turn][operator][side][slots] = zero
                 a_own[operator, turn, side, slots] = zero
 
     def table(column, off_at, count_at):
@@ -133,7 +132,7 @@
 
     def fine_rows(number, column, operators, load):
         flip_x = 1 - 2 * number
-        flip_y = 2 * lax.rem(column, 2) - 1
+        flip_y = 2 * (column % 2) - 1
 
         def p_block(off_x, off_y, corner_x, corner_y):
             return p_win[number + 1 + flip_x * off_x, column + 1 + flip_y * off_y, 2 * corner_x + corner_y]
@@ -182,32 +181,33 @@
                     1 + number, column + 1, 2 * corner_x + corner_y
                 ].T
 
-    def products(operator, number, places, start):
-        for place_n in range(5):
+    def products(operator, number, place_ns, start):
+        for place_n in place_ns:
             low = [0, 0, 0, 1, 3][place_n]
             high = [1, 3, 4, 4, 4][place_n]
-            right = jnp.concatenate(
-                [
-                    jnp.concatenate(
-                        [
-                            w_buf[operator, number, column, place_x, place_n - [0, 1, 1, 2][column]]
-                            for place_x in places
-                        ],
-                        axis=1,
-                    )
-                    for column in range(low, high)
-                ],
-                axis=0,
-            )
             left = lhs_t[number, :, low * size : high * size]
-            result = jnp.dot(left, right, preferred_element_type=F32)
-            for at, place_x in enumerate(places):
-                lanes = slice(at * size, (at + 1) * size)
-                if start:
-                    own[operator, place_x, place_n] = result[:size, lanes]
-                else:
-                    own[operator, place_x, place_n] += result[:size, lanes]
-                prod[operator, number, place_x, place_n] = result[size:, lanes].astype(BF16)
+            for places in ((0, 1), (2,)):
+                right = jnp.concatenate(
+                    [
+                        jnp.concatenate(
+                            [
+                                w_buf[operator, number, column, place_x, place_n - [0, 1, 1, 2][column]]
+                                for place_x in places
+                            ],
+                            axis=1,
+                        )
+                        for column in range(low, high)
+                    ],
+                    axis=0,
+                )
+                result = jnp.dot(left, right, preferred_element_type=F32)
+                for at, place_x in enumerate(places):
+                    lanes = slice(at * size, (at + 1) * size)
+                    if start:
+                        own[operator, place_n, place_x] = result[:size, lanes]
+                    else:
+                        own[operator, place_n, place_x] += result[:size, lanes]
+                    prod[operator, number, place_n, place_x] = result[size:, lanes].astype(BF16)
 
     def own_row(number):
         @pl.loop(0, 2)
@@ -225,15 +225,16 @@
             lambda operator, number, slot, column=column: off_ref[operator, number, column - 1, slot],
             lambda operator, number, column=column: count_ref[operator, number, column - 1],
         )
-    wait_col(6)
-    wait_col(7)
-    for side in range(2):
-        halo_table(side)
     for turn in range(2):
-        wait_col(turn)
-        for part in (1, 2):
-            row_copies[turn][part].start()
+        for side in range(2):
+            wait_col(turn, (side,))
+            row_copies[turn][1 + side].start()
         transposes(order[turn])
+        if turn == 0:
+            wait_col(6)
+            wait_col(7)
+            for side in range(2):
+                halo_table(side)
     for copies in row_copies:
         for copy in copies:
             copy.wait_recv()
@@ -243,22 +244,19 @@
         number = order[turn]
         own_row(number)
         for operator in range(2):
-            half = halves[turn][operator]
-            wait_col(2 + 2 * turn + operator)
-
-            @pl.loop(0, 2)
-            def _(side):
+            for side, place_ns in ((1, (3, 4)), (0, (0, 1, 2))):
+                half = halves[turn][operator][side]
+                wait_col(2 + 2 * turn + operator, (side,))
+
                 def load(operator, place):
-                    return half[side, slot_of[3 * side, operator * 2 + number, place]]
+                    return half[slot_of[3 * side, operator * 2 + number, place]]
 
                 fine_rows(number, 3 * side, (operator,), load)
-
-            for piece, places in enumerate(((0, 1), (2,))):
-                products(operator, number, places, turn == 0)
-                part = slice(places[0], places[-1] + 1)
+                products(operator, number, place_ns, turn == 0)
+                part = slice(place_ns[0], place_ns[-1] + 1)
                 copy = remote(
                     prod.at[operator, number, part], recv.at[operator, number, part],
-                    prod_send.at[operator, turn, piece], prod_recv.at[operator, number, piece], to_row(number),
+                    prod_send.at[operator, turn, side], prod_recv.at[operator, number, side], to_row(number),
                 )
                 copy.start()
                 prod_copies[operator].append(copy)
@@ -272,12 +270,12 @@
             for place in range(5):
                 total = None
                 if 1 <= place <= 3:
-                    total = own[operator, place - 1, place_n]
+                    total = own[operator, place_n, place - 1]
                 if place >= 2:
-                    term = recv[operator, 0, place - 2, place_n].astype(F32)
+                    term = recv[operator, 0, place_n, place - 2].astype(F32)
                     total = term if total is None else total + term
                 if place <= 2:
-                    term = recv[operator, 1, place, place_n].astype(F32)
+                    term = recv[operator, 1, place_n, place].astype(F32)
                     total = term if total is None else total + term
                 out_ref[operator, place, place_n] = total.astype(BF16)
 
@@ -305,7 +303,7 @@
             pltpu.VMEM((4, 6, 4) + block, BF16),
             pltpu.VMEM((2, 2, 2, slots + 1) + block, BF16),
         ]
-        + [pltpu.VMEM((2, slots + 1) + block, BF16)] * 4
+        + [pltpu.VMEM((slots + 1,) + block, BF16)] * 8
         + [
             pltpu.SMEM(a_off.shape, jnp.int32),
             pltpu.SMEM(a_count.shape, jnp.int32),
@@ -314,9 +312,9 @@
             pltpu.SMEM((4, 8, 128), jnp.int32),
             pltpu.VMEM((2, 2, 4, 3, 3) + block, BF16),
             pltpu.VMEM((2, 2 * size, 4 * size), BF16),
-            pltpu.VMEM((2, 3, 5) + block, F32),
-            pltpu.VMEM((2, 2, 3, 5) + block, BF16),
-            pltpu.VMEM((2, 2, 3, 5) + block, BF16),
+            pltpu.VMEM((2, 5, 3) + block, F32),
+            pltpu.VMEM((2, 2, 5, 3) + block, BF16),
+            pltpu.VMEM((2, 2, 5, 3) + block, BF16),
             pltpu.SemaphoreType.DMA((4,)),
             pltpu.SemaphoreType.DMA((2, 8)),
             pltpu.SemaphoreType.DMA((2, 8)),

time: 47.9 us -> 47.2 us (0.985)
  Pallas kernels: 46.6 us -> 46 us
    pallas_call x1, Pallas kernels: 46.6 us -> 46 us  [per_device(): pl.pallas_call(body, out_shape=jax.ShapeDtypeStruct((operators, 5, 5) + b...]
where the time goes in v3:
time: 47.2 us; the launch traced here: 47.1 us
  Pallas kernels  46 us (97%)
  local copies, waits for them, and re-layouts  1.17 us (2%)
    pallas_call x1, Pallas kernels, per_device(): pl.pallas_call(body, out_shape=jax.ShapeDtypeStruct((operators, 5, 5) + b...  46 us
    unnamed x1, local copies, waits for them, and re-layouts  1.17 us

profile of v3, /device:TPU:25, one launch (start us, length us, event | category | flops | bytes accessed | tf_op | source)
XLA Modules:
  0.0 47.1 jit_solution(11267954127732336895)
XLA Ops:
  0.0 46.0 %galerkin.1 = bf16[2,5,5,128,128]{4,3,2,1,0:T(8,128)(2,1)S(1)} custom-call(bf16[2,2,2,5,128,128]{5,4,3,2,1,0:T(8,128)(2,1)} %refs_0_.1, bf16[2,2,4,128,128]{4,3,2,1,0:T(8,128)(2,1)} %refs_1_.1, s32[2,2,2,5]{3,2,1,0:T(2,128)} %refs_2_.1, s32[2,2,2]{2,1,0:T(2,128)} %refs_3_.1), custom_call_target="tpu_custom_call" | custom-call | tf_op jit(solution)/shard_map/galerkin/pallas_call | solution.py:297
  46.0 1.2 %copy.7 = bf16[2,1,1,25,128,128]{5,4,3,2,1,0:T(8,128)(2,1)} copy(bf16[2,1,1,25,128,128]{5,4,3,2,1,0:T(8,128)(2,1)S(1)} %bitcast.3) | data formatting | bytes 3276800
